TPU v7x, 128 devices: a whole 4x4x4 slice. The times are simulated.
128 devices in a mesh: gx: 8 (over y_lo, x), gy: 16 (over y_hi, z, core).
Axes of the slice: x: 4, y: 4 (y_hi: 2, y_lo: 2; y = y_hi * 2 + y_lo), z: 4, core: 2. Of those that a mesh axis runs over, the one named last changes fastest.
Arguments:
- patches: bfloat16 [1024, 6144], P('gy', 'gx'), may hold values from -2000 to 2000
- norm_gain: float32 [6144], P('gx'), may hold values from 0.5 to 1.5
- w_up: bfloat16 [6144, 24576], P('gx', 'gy'), may hold values from -0.078125 to 0.078125
- bias_up: float32 [24576], P('gy'), may hold values from -4 to 4
- w_down: bfloat16 [24576, 6144], P('gy', 'gx'), may hold values from -0.0390625 to 0.0390625
- bias_down: float32 [6144], P('gx'), may hold values from -4 to 4
- cotangent: bfloat16 [1024, 6144], P('gy', 'gx'), may hold values from -4 to 4
Outputs:
- mlp_out: bfloat16 [1024, 6144], P('gy', 'gx')
- grad_patches: bfloat16 [1024, 6144], P('gy', 'gx')
- grad_gain: float32 [6144], P('gx')
- grad_w_up: float32 [6144, 24576], P('gx', 'gy')
- grad_bias_up: float32 [24576], P('gy')
- grad_w_down: float32 [24576, 6144], P('gy', 'gx')
- grad_bias_down: float32 [6144], P('gx')
All inputs are finite; a program needn't handle non-finite values.
Results may differ from a plain program's by a relative error of at most 0.007.
Values may be sent and summed in bfloat16 or wider, within the bound.
A program may use at most 128 MiB of HBM per device.

v0:
```python
import jax
import jax.numpy as jnp
from jax import lax
from jax.sharding import PartitionSpec as P

D = 6144
epsilon = 1e-06
inv_root_two = 0.7071067811865476
inv_root_two_pi = 0.3989422804014327


def gelu_value(hidden):
    return 0.5 * hidden * (1.0 + lax.erf(hidden * inv_root_two))


def gelu_slope(hidden):
    return (
        0.5 * (1.0 + lax.erf(hidden * inv_root_two))
        + hidden * jnp.exp(-0.5 * hidden * hidden) * inv_root_two_pi
    )


def over_rows(left, right):
    return lax.dot_general(
        left, right, (((0,), (0,)), ((), ())), preferred_element_type=jnp.float32
    )


def over_cols(left, right):
    return lax.dot_general(
        left, right, (((1,), (1,)), ((), ())), preferred_element_type=jnp.float32
    )


def shards(patches, norm_gain, w_up, bias_up, w_down, bias_down, cotangent):
    values = patches.astype(jnp.float32)
    row_total, row_squares = lax.psum(
        (jnp.sum(values, axis=1), jnp.sum(values * values, axis=1)), "gx"
    )
    row_mean = (row_total / D)[:, None]
    variance = (row_squares / D)[:, None] - row_mean * row_mean
    inv_std = lax.rsqrt(variance + epsilon)
    standard = (values - row_mean) * inv_std
    normed = (standard * norm_gain).astype(jnp.bfloat16)
    partial_value = jnp.dot(
        lax.all_gather(normed, "gy", axis=0, tiled=True), w_up, preferred_element_type=jnp.float32
    )
    hidden = lax.psum(partial_value, "gx") + bias_up
    act_whole = gelu_value(hidden).astype(jnp.bfloat16)
    block = act_whole
    mlp_out = (
        lax.psum_scatter(
            jnp.dot(block, w_down, preferred_element_type=jnp.float32),
            "gy",
            scatter_dimension=0,
            tiled=True,
        )
        + bias_down
    ).astype(jnp.bfloat16)
    piece = lax.all_gather(cotangent, "gy", axis=0, tiled=True)
    weight_total = over_rows(act_whole, piece)
    act_grads = over_cols(piece, w_down)
    grad_act = lax.psum(act_grads, "gx")
    grad_whole = (grad_act * gelu_slope(hidden)).astype(jnp.bfloat16)
    grad_bias_up = jnp.sum(grad_whole, axis=0, dtype=jnp.float32)
    grad_w_up = over_rows(lax.all_gather(normed, "gy", axis=0, tiled=True), grad_whole)
    block = grad_whole
    grad_normed = lax.psum_scatter(over_cols(block, w_up), "gy", scatter_dimension=0, tiled=True)
    grad_gain, grad_bias_down = lax.psum(
        (jnp.sum(grad_normed * standard, axis=0), jnp.sum(cotangent, axis=0, dtype=jnp.float32)),
        "gy",
    )
    scaled = grad_normed * norm_gain
    first_total, second_total = lax.psum(
        (jnp.sum(scaled, axis=1), jnp.sum(scaled * standard, axis=1)), "gx"
    )
    first_mean = (first_total / D)[:, None]
    second_mean = (second_total / D)[:, None]
    grad_patches = (inv_std * (scaled - first_mean - standard * second_mean)).astype(jnp.bfloat16)
    return (mlp_out, grad_patches, grad_gain, grad_w_up, grad_bias_up, weight_total, grad_bias_down)


def solution(mesh):
    in_specs = (
        P("gy", "gx"),
        P("gx"),
        P("gx", "gy"),
        P("gy"),
        P("gy", "gx"),
        P("gx"),
        P("gy", "gx"),
    )
    out_specs = (
        P("gy", "gx"),
        P("gy", "gx"),
        P("gx"),
        P("gx", "gy"),
        P("gy"),
        P("gy", "gx"),
        P("gx"),
    )
    return jax.shard_map(shards, mesh=mesh, in_specs=in_specs, out_specs=out_specs, check_vma=False)
```

profile of v0, /device:TPU:0, one launch (start us, length us, event | category | flops | bytes accessed | tf_op | source)
XLA Modules:
  0.0 570.0 jit_solution(7899502057630705862)
XLA Ops:
  7.2 0.0 all-gather.3.cloned.1.call-start
  7.2 1.2 convert_reduce_fusion.1
  8.4 19.8 %all-reduce.2 = (f32[64]{0:T(128)S(1)}, f32[64]{0:T(128)S(1)}) all-reduce(f32[64]{0:T(128)S(1)} %get-tuple-element.11, f32[64]{0:T(128)S(1)} %get-tuple-element.10), channel_id=1, replica_groups=mesh['gx'=8,'gy'=16] {'gx'}, use_global_device_ids=true, to_apply=%region_3.0 | all-reduce | flops 128 | bytes 1024 | tf_op jit(solution)/shard_map/psum | solution.py:37
  28.2 1.6 fusion.11
  29.9 0.0 all-gather.3.cloned.1.call-update
  29.9 0.0 all-gather.5.cloned.1.call-start
  29.9 0.7 all-gather.5.cloned.1.call-update
  30.6 0.0 all-reduce.6.cloned.1.call-start
  30.7 45.4 %all-gather.3.cloned.1.call-done = bf16[1024,768]{1,0:T(8,128)(2,1)} async-done(((bf16[64,768]{1,0:T(8,128)(2,1)}), bf16[1024,768]{1,0:T(8,128)(2,1)}) %all-gather.3.cloned.1.call-update) | async-done | bytes 1572880 | tf_op jit(solution)/shard_map/all_gather | solution.py:46
  76.0 5.9 %fusion.19 = f32[1024,1536]{1,0:T(8,128)} fusion(bf16[1024,768]{1,0:T(8,128)(2,1)} %all-gather.3.cloned.1.call-done, bf16[768,1536]{1,0:T(8,128)(2,1)S(1)} %copy-done), kind=kOutput, calls=%fused_computation.32 | convolution fusion | flops 2415919104 | bytes 10223616 | tf_op jit(solution)/shard_map/dot_general | solution.py:45
  81.9 41.7 %all-gather.5.cloned.1.call-done = bf16[1024,768]{1,0:T(8,128)(2,1)} async-done(((bf16[64,768]{1,0:T(8,128)(2,1)}), bf16[1024,768]{1,0:T(8,128)(2,1)}) %all-gather.5.cloned.1.call-update) | async-done | bytes 1572880 | tf_op jit(solution)/shard_map/all_gather | solution.py:60
  123.6 7.4 %fusion.21 = f32[1024,1536]{1,0:T(8,128)} fusion(bf16[1024,768]{1,0:T(8,128)(2,1)} %all-gather.5.cloned.1.call-done, bf16[1536,768]{1,0:T(8,128)(2,1)} %param.11), kind=kOutput, calls=%fused_computation.34 | convolution fusion | flops 2415919104 | bytes 10223616 | tf_op jit(solution)/shard_map/dot_general | solution.py:30
  131.0 0.0 all-reduce.6.cloned.1.call-update
  131.0 0.0 reduce-scatter.5.cloned.1.call-start
  131.1 262.5 %all-reduce.6.cloned.1.call-done = (f32[1024,1536]{1,0:T(8,128)}, f32[1024,1536]{1,0:T(8,128)}) async-done(((f32[1024,1536]{1,0:T(8,128)}, f32[1024,1536]{1,0:T(8,128)}), (f32[1024,1536]{1,0:T(8,128)}, f32[1024,1536]{1,0:T(8,128)})) %all-reduce.6.cloned.1.call-update) | async-done | bytes 12582928 | tf_op jit(solution)/shard_map/psum | solution.py:48
  393.6 9.2 %convert_reduce_fusion = (f32[1536]{0:T(1024)}, bf16[1024,1536]{1,0:T(8,128)(2,1)S(1)}, bf16[1024,1536]{1,0:T(8,128)(2,1)}) fusion(f32[1024,1536]{1,0:T(8,128)} %get-tuple-element.19, f32[1024,1536]{1,0:T(8,128)} %get-tuple-element.18, f32[1536]{0:T(1024)S(1)} %copy-done.6), kind=kLoop, calls=%fused_computation.7 | loop fusion | flops 25164288 | bytes 18886656 | tf_op jit(solution)/shard_map/reduce_sum | solution.py:65
  402.8 1.7 copy-done.1
  404.5 4.3 fusion.22
  408.8 0.0 reduce-scatter.5.cloned.1.call-update
  408.8 0.0 reduce-scatter.3.cloned.1.call-start
  408.9 6.9 %fusion.20 = f32[1024,768]{1,0:T(8,128)} fusion(bf16[1024,1536]{1,0:T(8,128)(2,1)} %get-tuple-element.22, bf16[1536,768]{1,0:T(8,128)(2,1)} %param.11), kind=kOutput, calls=%fused_computation.33 | convolution fusion | flops 2415919104 | bytes 8650752 | tf_op jit(solution)/shard_map/dot_general | solution.py:53
  415.8 0.0 reduce-scatter.3.cloned.1.call-update
  415.8 0.9 copy-done.4
  416.7 7.5 %fusion.23 = f32[768,1536]{1,0:T(8,128)} fusion(bf16[1024,768]{1,0:T(8,128)(2,1)} %all-gather.3.cloned.1.call-done, bf16[1024,1536]{1,0:T(8,128)(2,1)} %copy-done.1), kind=kOutput, calls=%fused_computation.36 | convolution fusion | flops 2415919104 | bytes 9437184 | tf_op jit(solution)/shard_map/dot_general | solution.py:24
  424.3 4.4 fusion.24
  428.6 54.9 %reduce-scatter.5.cloned.1.call-done = f32[64,768]{1,0:T(8,128)} async-done(((f32[1024,768]{1,0:T(8,128)}), f32[64,768]{1,0:T(8,128)}) %reduce-scatter.5.cloned.1.call-update) | async-done | bytes 196624 | tf_op jit(solution)/shard_map/reduce_scatter | solution.py:68
  483.5 1.2 fusion.16
  484.7 18.7 %all-reduce.1 = (f32[64]{0:T(128)S(1)}, f32[64]{0:T(128)S(1)}) all-reduce(f32[64]{0:T(128)S(1)} %get-tuple-element.8, f32[64]{0:T(128)S(1)} %get-tuple-element.9), channel_id=1, replica_groups=mesh['gx'=8,'gy'=16] {'gx'}, use_global_device_ids=true, to_apply=%region_11.0 | all-reduce | flops 128 | bytes 1024 | tf_op jit(solution)/shard_map/psum | solution.py:74
  503.3 34.6 %all-reduce = (f32[768]{0:T(1024)}, f32[768]{0:T(1024)}) all-reduce(f32[768]{0:T(1024)S(1)} %get-tuple-element.7, f32[768]{0:T(1024)S(1)} %convert_reduce_fusion.2), channel_id=1, replica_groups=mesh['gx'=8,'gy'=16] {'gy'}, use_global_device_ids=true, to_apply=%region_13.0 | all-reduce | flops 1536 | bytes 12288 | tf_op jit(solution)/shard_map/psum | solution.py:69
  538.0 1.7 fusion.15
  539.7 22.2 %reduce-scatter.3.cloned.1.call-done = f32[64,768]{1,0:T(8,128)} async-done(((f32[1024,768]{1,0:T(8,128)}), f32[64,768]{1,0:T(8,128)}) %reduce-scatter.3.cloned.1.call-update) | async-done | bytes 196624 | tf_op jit(solution)/shard_map/reduce_scatter | solution.py:52
  561.9 1.6 add_convert_fusion
  (19 shorter events, 0.1 us)
Async XLA Ops:
  7.2 68.9 %copy-start = (bf16[768,1536]{1,0:T(8,128)(2,1)S(1)}, bf16[768,1536]{1,0:T(8,128)(2,1)}, u32[]{:S(2)}) copy-start(bf16[768,1536]{1,0:T(8,128)(2,1)} %param.9) | copy-start | bytes 7077892
  7.2 68.9 %all-gather.3.cloned.1.call-start = ((), (), s32[]{:S(2)}) async-start(), calls=%async_computation.2 | async-start | bytes 1671168 | tf_op jit(solution)/shard_map/all_gather | solution.py:46
  29.9 93.8 %all-gather.5.cloned.1.call-start = ((), (), s32[]{:S(2)}) async-start(), calls=%async_computation.4 | async-start | bytes 1671168 | tf_op jit(solution)/shard_map/all_gather | solution.py:60
  30.6 363.0 %all-reduce.6.cloned.1.call-start = ((), (), s32[]{:S(2)}) async-start(), calls=%async_computation.6 | async-start | bytes 25165824 | tf_op jit(solution)/shard_map/psum | solution.py:48
  131.0 262.6 %copy-start.6 = (f32[1536]{0:T(1024)S(1)}, f32[1536]{0:T(1024)}, u32[]{:S(2)}) copy-start(f32[1536]{0:T(1024)} %param.10) | copy-start | bytes 18436
  131.0 352.5 %reduce-scatter.5.cloned.1.call-start = ((), (), s32[]{:S(2)}) async-start(), calls=%async_computation.5 | async-start | bytes 3342336 | tf_op jit(solution)/shard_map/reduce_scatter | solution.py:68
  402.8 1.7 copy-start.1
  408.8 153.1 %reduce-scatter.3.cloned.1.call-start = ((), (), s32[]{:S(2)}) async-start(), calls=%async_computation.3 | async-start | bytes 3342336 | tf_op jit(solution)/shard_map/reduce_scatter | solution.py:52
  415.8 0.9 copy-start.4
  416.7 7.5 %copy-start.2 = (bf16[1024,1536]{1,0:T(8,128)(2,1)S(1)}, bf16[1024,1536]{1,0:T(8,128)(2,1)}, u32[]{:S(2)}) copy-start(bf16[1024,1536]{1,0:T(8,128)(2,1)} %get-tuple-element.22) | copy-start | bytes 9437188
  416.7 7.5 %copy-start.8 = (bf16[1024,768]{1,0:T(8,128)(2,1)S(1)}, bf16[1024,768]{1,0:T(8,128)(2,1)}, u32[]{:S(2)}) copy-start(bf16[1024,768]{1,0:T(8,128)(2,1)} %all-gather.5.cloned.1.call-done) | copy-start | bytes 4718596
  424.2 59.3 %copy-start.3 = (bf16[64,768]{1,0:T(8,128)(2,1)S(1)}, bf16[64,768]{1,0:T(8,128)(2,1)}, u32[]{:S(2)}) copy-start(bf16[64,768]{1,0:T(8,128)(2,1)} %param.7) | copy-start | bytes 294916
  424.2 59.3 %copy-start.5 = (f32[768]{0:T(1024)S(1)}, f32[768]{0:T(1024)}, u32[]{:S(2)}) copy-start(f32[768]{0:T(1024)} %param.8) | copy-start | bytes 9220
  424.2 137.7 %copy-start.7 = (f32[768]{0:T(1024)S(1)}, f32[768]{0:T(1024)}, u32[]{:S(2)}) copy-start(f32[768]{0:T(1024)} %param.12) | copy-start | bytes 9220
Sparse Core Ops, SparseCore 0:
  30.0 45.9 all-gather.2
  78.5 45.0 all-gather.4
  131.2 262.3 all-reduce.5
  408.9 74.5 reduce-scatter.4
  487.4 74.4 reduce-scatter.2
where the time goes:
time: 570 us
  waiting for transfers between devices  427 us (75%)
  blocking collectives  73.1 us (13%)
  matrix products  36.4 us (6%)
  other arithmetic  16.4 us (3%)
  between operations  13.8 us (2%)
    psum x1, waiting for transfers between devices, shards(): hidden = lax.psum(partial_value, 'gx') + bias_up  263 us
    reduce_scatter x1, waiting for transfers between devices, shards(): lax.psum_scatter(over_cols(block, w_up), 'gy', scatter_dimension=0, tiled...  54.9 us
    all_gather x1, waiting for transfers between devices, shards(): lax.all_gather(normed, 'gy', axis=0, tiled=True)  45.4 us
    all_gather x1, waiting for transfers between devices, shards(): piece = lax.all_gather(cotangent, 'gy', axis=0, tiled=True)  41.7 us
    psum x1, blocking collectives, shards(): lax.psum((jnp.sum(grad_normed * standard, axis=0), jnp.sum(cotangent, axi...  34.6 us
    reduce_scatter x1, waiting for transfers between devices, shards(): lax.psum_scatter(jnp.dot(block, w_down, preferred_element_type=jnp.float3...  22.2 us
    psum x1, blocking collectives, shards(): lax.psum((jnp.sum(values, axis=1), jnp.sum(values * values, axis=1)), 'gx')  19.8 us
    psum x1, blocking collectives, shards(): lax.psum((jnp.sum(scaled, axis=1), jnp.sum(scaled * standard, axis=1)), '...  18.7 us
  transfers between devices with their start and end apart: 5, of which 5 were waited for; matrix products, arithmetic and copies ran while one was open for 5% of the time, Pallas kernels for 0%

commit v1 on v0

--- a/solution.py
+++ b/solution.py
@@ -45,7 +45,7 @@
     partial_value = jnp.dot(
         lax.all_gather(normed, "gy", axis=0, tiled=True), w_up, preferred_element_type=jnp.float32
     )
-    hidden = lax.psum(partial_value, "gx") + bias_up
+    hidden = jnp.sum(lax.all_gather(partial_value, "gx"), axis=0) + bias_up
     act_whole = gelu_value(hidden).astype(jnp.bfloat16)
     block = act_whole
     mlp_out = (

time: 570 us -> 932 us (1.64)
  waiting for transfers between devices: 427 us -> 766 us
  other arithmetic: 16.4 us -> 38.7 us
    all_gather x0 -> x1, waiting for transfers between devices: none -> 478 us  [shards(): hidden = jnp.sum(lax.all_gather(partial_value, 'gx'), axis=0) + bias_up]
    psum x1, waiting for transfers between devices: 263 us -> 124 us  [shards(): grad_act = lax.psum(act_grads, 'gx')]
    reduce_sum x0 -> x1, other arithmetic: none -> 22.3 us  [shards(): hidden = jnp.sum(lax.all_gather(partial_value, 'gx'), axis=0) + bias_up]
  transfers between devices with their start and end apart: 5 -> 6, of which waited for: 5 -> 6; matrix products, arithmetic and copies ran while one was open for 5% -> 6% of each run, Pallas kernels for 0% -> 0%
where the time goes in v1:
time: 932 us
  waiting for transfers between devices  766 us (82%)
  blocking collectives  73.2 us (8%)
  other arithmetic  38.7 us (4%)
  matrix products  36.4 us (4%)
  between operations  14.2 us (2%)
    all_gather x1, waiting for transfers between devices, shards(): hidden = jnp.sum(lax.all_gather(partial_value, 'gx'), axis=0) + bias_up  478 us
    psum x1, waiting for transfers between devices, shards(): grad_act = lax.psum(act_grads, 'gx')  124 us
    reduce_scatter x1, waiting for transfers between devices, shards(): lax.psum_scatter(over_cols(block, w_up), 'gy', scatter_dimension=0, tiled...  54.6 us
    all_gather x1, waiting for transfers between devices, shards(): lax.all_gather(normed, 'gy', axis=0, tiled=True)  45.4 us
    all_gather x1, waiting for transfers between devices, shards(): piece = lax.all_gather(cotangent, 'gy', axis=0, tiled=True)  41.7 us
    psum x1, blocking collectives, shards(): lax.psum((jnp.sum(grad_normed * standard, axis=0), jnp.sum(cotangent, axi...  34.7 us
    reduce_sum x1, other arithmetic, shards(): hidden = jnp.sum(lax.all_gather(partial_value, 'gx'), axis=0) + bias_up  22.3 us
    reduce_scatter x1, waiting for transfers between devices, shards(): lax.psum_scatter(jnp.dot(block, w_down, preferred_element_type=jnp.float3...  22.2 us
  transfers between devices with their start and end apart: 6, of which 6 were waited for; matrix products, arithmetic and copies ran while one was open for 6% of the time, Pallas kernels for 0%

profile of v1, /device:TPU:0, one launch (start us, length us, event | category | flops | bytes accessed | tf_op | source)
XLA Modules:
  0.0 931.7 jit_solution(6520909556004952064)
XLA Ops:
  7.2 0.0 all-gather.5.cloned.1.call-start
  7.2 1.2 convert_reduce_fusion.1
  8.4 19.8 %all-reduce.2 = (f32[64]{0:T(128)S(1)}, f32[64]{0:T(128)S(1)}) all-reduce(f32[64]{0:T(128)S(1)} %get-tuple-element.11, f32[64]{0:T(128)S(1)} %get-tuple-element.10), channel_id=1, replica_groups=mesh['gx'=8,'gy'=16] {'gx'}, use_global_device_ids=true, to_apply=%region_3.0 | all-reduce | flops 128 | bytes 1024 | tf_op jit(solution)/shard_map/psum | solution.py:37
  28.2 1.6 fusion.11
  29.9 0.0 all-gather.5.cloned.1.call-update
  29.9 0.0 all-gather.7.cloned.1.call-start
  29.9 0.7 all-gather.7.cloned.1.call-update
  30.6 0.0 all-gather.9.cloned.1.call-start
  30.7 45.4 %all-gather.5.cloned.1.call-done = bf16[1024,768]{1,0:T(8,128)(2,1)} async-done(((bf16[64,768]{1,0:T(8,128)(2,1)}), bf16[1024,768]{1,0:T(8,128)(2,1)}) %all-gather.5.cloned.1.call-update) | async-done | bytes 1572880 | tf_op jit(solution)/shard_map/all_gather | solution.py:46
  76.0 5.9 fusion.19
  81.9 0.0 all-reduce.5.cloned.1.call-start
  82.0 41.7 %all-gather.7.cloned.1.call-done = bf16[1024,768]{1,0:T(8,128)(2,1)} async-done(((bf16[64,768]{1,0:T(8,128)(2,1)}), bf16[1024,768]{1,0:T(8,128)(2,1)}) %all-gather.7.cloned.1.call-update) | async-done | bytes 1572880 | tf_op jit(solution)/shard_map/all_gather | solution.py:60
  123.6 7.4 fusion.21
  131.0 0.0 reduce-scatter.5.cloned.1.call-start
  131.1 478.0 %all-gather.9.cloned.1.call-done = f32[8192,1536]{1,0:T(8,128)} async-done(((f32[1024,1536]{1,0:T(8,128)}), f32[8192,1536]{1,0:T(8,128)}) %all-gather.9.cloned.1.call-update) | async-done | bytes 50331664 | tf_op jit(solution)/shard_map/all_gather | solution.py:48
  609.1 22.3 %reduce_sum.74 = f32[1024,1536]{1,0:T(8,128)} reduce(f32[8,1024,1536]{2,1,0:T(8,128)} %bitcast.13, f32[]{:T(128)} %constant.4.clone.1), dimensions={0}, to_apply=%region_4.0 | reduce | flops 11010048 | bytes 56623108 | tf_op jit(solution)/shard_map/reduce_sum | solution.py:48
  631.4 123.7 %all-reduce.5.cloned.1.call-done = f32[1024,1536]{1,0:T(8,128)} async-done(((f32[1024,1536]{1,0:T(8,128)}), f32[1024,1536]{1,0:T(8,128)}) %all-reduce.5.cloned.1.call-update) | async-done | bytes 6291472 | tf_op jit(solution)/shard_map/psum | solution.py:63
  755.1 9.2 convert_reduce_fusion
  764.3 1.7 copy-done.1
  766.0 4.3 fusion.22
  770.4 0.2 reduce-scatter.3.cloned.1.call-start
  770.6 6.9 fusion.20
  777.5 0.9 copy-done.4
  778.4 7.5 fusion.23
  786.0 4.4 fusion.24
  790.4 54.6 %reduce-scatter.5.cloned.1.call-done = f32[64,768]{1,0:T(8,128)} async-done(((f32[1024,768]{1,0:T(8,128)}), f32[64,768]{1,0:T(8,128)}) %reduce-scatter.5.cloned.1.call-update) | async-done | bytes 196624 | tf_op jit(solution)/shard_map/reduce_scatter | solution.py:68
  844.9 1.2 fusion.16
  846.1 18.7 %all-reduce.1 = (f32[64]{0:T(128)S(1)}, f32[64]{0:T(128)S(1)}) all-reduce(f32[64]{0:T(128)S(1)} %get-tuple-element.8, f32[64]{0:T(128)S(1)} %get-tuple-element.9), channel_id=1, replica_groups=mesh['gx'=8,'gy'=16] {'gx'}, use_global_device_ids=true, to_apply=%region_11.0 | all-reduce | flops 128 | bytes 1024 | tf_op jit(solution)/shard_map/psum | solution.py:74
  864.8 34.7 %all-reduce = (f32[768]{0:T(1024)}, f32[768]{0:T(1024)}) all-reduce(f32[768]{0:T(1024)S(1)} %get-tuple-element.7, f32[768]{0:T(1024)S(1)} %convert_reduce_fusion.2), channel_id=1, replica_groups=mesh['gx'=8,'gy'=16] {'gy'}, use_global_device_ids=true, to_apply=%region_13.0 | all-reduce | flops 1536 | bytes 12288 | tf_op jit(solution)/shard_map/psum | solution.py:69
  899.4 1.7 fusion.15
  901.1 22.2 %reduce-scatter.3.cloned.1.call-done = f32[64,768]{1,0:T(8,128)} async-done(((f32[1024,768]{1,0:T(8,128)}), f32[64,768]{1,0:T(8,128)}) %reduce-scatter.3.cloned.1.call-update) | async-done | bytes 196624 | tf_op jit(solution)/shard_map/reduce_scatter | solution.py:52
  923.3 1.6 add_convert_fusion
  (23 shorter events, 0.1 us)
Async XLA Ops:
  7.2 68.9 %copy-start = (bf16[768,1536]{1,0:T(8,128)(2,1)S(1)}, bf16[768,1536]{1,0:T(8,128)(2,1)}, u32[]{:S(2)}) copy-start(bf16[768,1536]{1,0:T(8,128)(2,1)} %param.9) | copy-start | bytes 7077892
  7.2 68.9 %all-gather.5.cloned.1.call-start = ((), (), s32[]{:S(2)}) async-start(), calls=%async_computation.2 | async-start | bytes 1671168 | tf_op jit(solution)/shard_map/all_gather | solution.py:46
  29.9 93.8 %all-gather.7.cloned.1.call-start = ((), (), s32[]{:S(2)}) async-start(), calls=%async_computation.4 | async-start | bytes 1671168 | tf_op jit(solution)/shard_map/all_gather | solution.py:60
  30.6 578.5 %all-gather.9.cloned.1.call-start = ((), (), s32[]{:S(2)}) async-start(), calls=%async_computation.7 | async-start | bytes 56623104 | tf_op jit(solution)/shard_map/all_gather | solution.py:48
  81.9 673.2 %all-reduce.5.cloned.1.call-start = ((), (), s32[]{:S(2)}) async-start(), calls=%async_computation.5 | async-start | bytes 12582912 | tf_op jit(solution)/shard_map/psum | solution.py:63
  131.0 713.9 %reduce-scatter.5.cloned.1.call-start = ((), (), s32[]{:S(2)}) async-start(), calls=%async_computation.6 | async-start | bytes 3342336 | tf_op jit(solution)/shard_map/reduce_scatter | solution.py:68
  609.1 146.0 %copy-start.6 = (f32[1536]{0:T(1024)S(1)}, f32[1536]{0:T(1024)}, u32[]{:S(2)}) copy-start(f32[1536]{0:T(1024)} %param.10) | copy-start | bytes 18436
  764.3 1.7 copy-start.1
  770.4 152.9 %reduce-scatter.3.cloned.1.call-start = ((), (), s32[]{:S(2)}) async-start(), calls=%async_computation.3 | async-start | bytes 3342336 | tf_op jit(solution)/shard_map/reduce_scatter | solution.py:52
  777.5 0.9 copy-start.4
  778.4 7.5 copy-start.2
  778.4 7.5 copy-start.8
  785.9 59.0 %copy-start.3 = (bf16[64,768]{1,0:T(8,128)(2,1)S(1)}, bf16[64,768]{1,0:T(8,128)(2,1)}, u32[]{:S(2)}) copy-start(bf16[64,768]{1,0:T(8,128)(2,1)} %param.7) | copy-start | bytes 294916
  786.0 59.0 %copy-start.5 = (f32[768]{0:T(1024)S(1)}, f32[768]{0:T(1024)}, u32[]{:S(2)}) copy-start(f32[768]{0:T(1024)} %param.8) | copy-start | bytes 9220
  786.0 137.3 %copy-start.7 = (f32[768]{0:T(1024)S(1)}, f32[768]{0:T(1024)}, u32[]{:S(2)}) copy-start(f32[768]{0:T(1024)} %param.12) | copy-start | bytes 9220
Sparse Core Ops, SparseCore 0:
  30.0 45.9 all-gather.4
  78.5 45.0 all-gather.6
  125.3 483.7 all-gather.8
  611.5 143.5 all-reduce.4
  770.5 74.3 reduce-scatter.4
  848.8 74.4 reduce-scatter.2
